TPU v7x, 32 devices: a whole 2x2x4 slice. The times are simulated.
32 devices in a mesh: sub: 8 (over y, x, core), rep: 4 (over z).
Axes of the slice: x: 2, y: 2, z: 4, core: 2. Of those that a mesh axis runs over, the one named last changes fastest.
Arguments:
- loads: bfloat16 [64, 256, 1024], P('sub', 'rep'), may hold values from -6 to 6
- operators: bfloat16 [64, 1024, 1024], P('sub'), may hold values from -0.1875 to 0.1875
- owner: int32 [512, 1], P('sub'), may hold values from 0 to 7; in each aligned block of 64 rows (0 to 63, 64 to 127, ...) at most 16 rows name the same one
- dual_block: int32 [512], P('sub'), may hold values from 0 to 15
- scale_index: int32 [16384], P('sub'), may hold values from 0 to 3
- basis: bfloat16 [16384, 1024], P('sub'), may hold values from -0.046875 to 0.046875
- coarse: bfloat16 [1024, 1024], replicated, may hold values from -0.75 to 0.75
Outputs:
- start: float32 [256, 16384], P('rep', 'sub')
- resid: float32 [256, 16384], P('rep', 'sub')
Inputs may be any that keep to these rules, and one draw needn't show every extreme that they name: Among the blocks of the subdomains of one index of sub (aligned blocks of 64 rows), no owner is named more than 16 times, a bound that some block reaches.
All inputs are finite; a program needn't handle non-finite values.
Results may differ from a plain program's by a relative error of at most 0.0075.
Values may be sent and summed in bfloat16 or wider, within the bound.
A program may use at most 128 MiB of HBM per device.

v0:
```python
import jax
import jax.numpy as jnp
from jax import lax
from jax.sharding import PartitionSpec as P

BLK = 128


def apply_local(inputs, operators):
    return jnp.einsum("skl,slm->skm", inputs, operators, preferred_element_type=jnp.float32).astype(
        jnp.bfloat16
    )


def make_blocks(values, width):
    count, columns, local = values.shape
    return (
        values.reshape(count, columns, local // width, width)
        .transpose(0, 2, 1, 3)
        .reshape(-1, columns, width)
    )


def from_blocks(blocks, count):
    total, columns, width = blocks.shape
    per_sub = total // count
    return (
        blocks.reshape(count, per_sub, columns, width)
        .transpose(0, 2, 1, 3)
        .reshape(count, columns, per_sub * width)
    )


def pack_slots(blocks, dests, ranks, peers, slots):
    columns, width = (blocks.shape[1], blocks.shape[2])
    return jnp.zeros((peers, slots, columns, width), jnp.bfloat16).at[dests, ranks].set(blocks)


def accumulate(received, got_ids, own_blocks, weight):
    columns, width = (received.shape[2], received.shape[3])
    flat = received.reshape(-1, columns, width).astype(jnp.float32)
    total = jnp.zeros((own_blocks, columns, width), jnp.float32).at[got_ids.reshape(-1)].add(flat)
    return total.transpose(1, 0, 2).reshape(columns, own_blocks * width) * weight[None, :]


def per_device(loads, operators, owner, dual_block, scale_index, basis, coarse):
    sub_count = loads.shape[0]
    width = BLK
    peers = lax.axis_size("sub")
    dests = owner[:, 0]
    nblocks = dests.shape[0]
    slots = max(2, 2 * nblocks // peers)
    own_blocks = basis.shape[0] // width
    positions = jnp.arange(nblocks, dtype=jnp.int32)
    earlier = positions[None, :] < positions[:, None]
    same = dests[None, :] == dests[:, None]
    ranks = jnp.sum(jnp.logical_and(earlier, same), axis=1)
    weight = 1.0 / (1.0 + scale_index.astype(jnp.float32))
    terms = apply_local(loads, operators)
    packed = pack_slots(make_blocks(terms, width), dests, ranks, peers, slots)
    id_slots = jnp.zeros((peers, slots), jnp.int32).at[dests, ranks].set(dual_block)
    received, got_ids = (
        lax.all_to_all(packed, "sub", split_axis=0, concat_axis=0, tiled=True),
        lax.all_to_all(id_slots, "sub", split_axis=0, concat_axis=0, tiled=True),
    )
    dual = accumulate(received, got_ids, own_blocks, weight)
    coeff = jnp.dot(dual.astype(jnp.bfloat16), basis, preferred_element_type=jnp.float32)
    summed = lax.psum(coeff, "sub")
    solved = jnp.dot(
        summed.astype(jnp.bfloat16), coarse, preferred_element_type=jnp.float32
    ).astype(jnp.bfloat16)
    start = lax.dot_general(
        solved, basis, (((1,), (1,)), ((), ())), preferred_element_type=jnp.float32
    )
    columns = start.shape[0]
    start_blocks = start.astype(jnp.bfloat16).reshape(columns, own_blocks, width).transpose(1, 0, 2)
    requested = start_blocks[got_ids]
    returned = lax.all_to_all(requested, "sub", split_axis=0, concat_axis=0, tiled=True)
    picked = returned[dests, ranks]
    local = from_blocks(picked, sub_count)
    again = apply_local(local, operators)
    received_again = lax.all_to_all(
        pack_slots(make_blocks(again, width), dests, ranks, peers, slots),
        "sub",
        split_axis=0,
        concat_axis=0,
        tiled=True,
    )
    applied = accumulate(received_again, got_ids, own_blocks, weight)
    return (start, dual - applied)


def solution(mesh):
    return jax.shard_map(
        per_device,
        mesh=mesh,
        in_specs=(
            P("sub", "rep", None),
            P("sub", None, None),
            P("sub", None),
            P("sub"),
            P("sub"),
            P("sub", None),
            P(),
        ),
        out_specs=(P("rep", "sub"), P("rep", "sub")),
        check_vma=False,
    )
```

profile of v0, /device:TPU:0, one launch (start us, length us, event | category | flops | bytes accessed | tf_op | source)
XLA Modules:
  0.0 227.0 jit_solution(12576725481000014355)
XLA Ops:
  0.6 1.0 convert_reduce_fusion
  2.9 10.2 %scatter_fusion = s32[8,16]{1,0:T(8,128)} fusion(s32[8,16]{1,0:T(8,128)} %broadcast.75, s32[64]{0:T(128)S(1)} %get-tuple-element.2, s32[64]{0:T(128)} %param.10), kind=kCustom, calls=%fused_computation.2 | custom fusion | bytes 1280 | tf_op jit(solution)/shard_map/scatter | solution.py:61
  13.1 5.2 %all-to-all-start = ((s32[8,1,16]{2,1,0:T(1,128)}), s32[8,1,16]{2,1,0:T(1,128)S(1)}, u32[]{:S(2)}, u32[]{:S(2)}) async-start(s32[8,1,16]{2,1,0:T(1,128)} %bitcast.4), calls=%async_computation | async-start | bytes 8192 | tf_op jit(solution)/shard_map/all_to_all | solution.py:64
  18.3 9.1 %fusion = bf16[8,8,8,8,128]{4,3,2,1,0:T(8,128)(2,1)S(1)} fusion(bf16[8,64,1024]{2,1,0:T(8,128)(2,1)} %param.7, bf16[8,1024,1024]{2,1,0:T(8,128)(2,1)} %param.8), kind=kOutput, calls=%fused_computation.11 | convolution fusion | flops 1074266112 | bytes 18874368 | tf_op jit(solution)/shard_map/skl,slm->skm/dot_general | solution.py:10
  27.7 1.9 broadcast.81.clone
  29.6 8.9 %scatter_fusion.1 = bf16[8,16,64,128]{3,2,1,0:T(8,128)(2,1)} fusion(bf16[8,16,64,128]{3,2,1,0:T(8,128)(2,1)} %broadcast.81.clone, s32[64]{0:T(128)S(1)} %get-tuple-element.2, bf16[64,64,128]{2,1,0:T(8,128)(2,1)S(1)} %bitcast.87), kind=kCustom, calls=%fused_computation.3 | custom fusion | bytes 3146240 | tf_op jit(solution)/shard_map/scatter | solution.py:36
  38.5 4.5 %all-to-all-start.1 = ((bf16[8,16,64,128]{3,2,1,0:T(8,128)(2,1)}), bf16[8,16,64,128]{3,2,1,0:T(8,128)(2,1)}, u32[]{:S(2)}, u32[]{:S(2)}) async-start(bf16[8,16,64,128]{3,2,1,0:T(8,128)(2,1)} %scatter_fusion.1), calls=%async_computation.1 | async-start | bytes 4194304 | tf_op jit(solution)/shard_map/all_to_all | solution.py:63
  44.4 25.3 %all-to-all-done.1 = bf16[8,16,64,128]{3,2,1,0:T(8,128)(2,1)} async-done(((bf16[8,16,64,128]{3,2,1,0:T(8,128)(2,1)}), bf16[8,16,64,128]{3,2,1,0:T(8,128)(2,1)}, u32[]{:S(2)}, u32[]{:S(2)}) %all-to-all-start.1) | async-done | bytes 2097184 | tf_op jit(solution)/shard_map/all_to_all | solution.py:63
  69.6 4.0 %bitcast_convert_fusion.1 = f32[128,64,128]{2,1,0:T(8,128)} fusion(bf16[8,16,64,128]{3,2,1,0:T(8,128)(2,1)} %all-to-all-done.1), kind=kLoop, calls=%fused_computation.8 | loop fusion | flops 1048576 | bytes 6291456 | tf_op jit(solution)/shard_map/convert_element_type | solution.py:41
  73.6 13.6 %scatter_fusion.2 = f32[16,64,128]{2,1,0:T(8,128)S(1)} fusion(f32[16,64,128]{2,1,0:T(8,128)S(1)} %broadcast.74.clone, s32[128]{0:T(128)S(1)} %fusion.14, f32[128,64,128]{2,1,0:T(8,128)} %bitcast_convert_fusion.1), kind=kCustom, calls=%fused_computation.4 | custom fusion | flops 1048576 | bytes 12583424 | tf_op jit(solution)/shard_map/scatter-add | solution.py:42
  87.2 3.0 %fusion.7 = f32[64,1024]{1,0:T(8,128)S(1)} fusion(bf16[2048,1024]{1,0:T(8,128)(2,1)} %param.12, f32[2048]{0:T(1024)S(1)} %add_divide_fusion, f32[16,64,128]{2,1,0:T(8,128)S(1)} %scatter_fusion.2), kind=kOutput, calls=%fused_computation.23 | convolution fusion | flops 268697600 | bytes 4988928 | tf_op jit(solution)/shard_map/dot_general | solution.py:67
  90.3 25.4 %all-reduce.1 = bf16[64,1024]{1,0:T(8,128)(2,1)S(1)} all-reduce(f32[64,1024]{1,0:T(8,128)S(1)} %fusion.7), channel_id=1, replica_groups=mesh['sub'=8,'rep'=4] {'sub'}, use_global_device_ids=true, to_apply=%region_4.0 | all-reduce | flops 65536 | bytes 393216 | tf_op jit(solution)/shard_map/psum | solution.py:68
  115.7 4.8 %fusion.2 = f32[64,2048]{1,0:T(8,128)} fusion(bf16[2048,1024]{1,0:T(8,128)(2,1)} %param.12, bf16[1024,1024]{1,0:T(8,128)(2,1)S(1)} %copy-done, bf16[64,1024]{1,0:T(8,128)(2,1)S(1)} %all-reduce.1), kind=kOutput, calls=%fused_computation.14 | convolution fusion | flops 402718720 | bytes 6946816 | tf_op jit(solution)/shard_map/dot_general | solution.py:72
  120.4 1.1 bitcast_bitcast_fusion
  121.5 2.1 gather_fusion
  123.6 30.9 %all_to_all.27 = bf16[8,16,64,128]{3,2,1,0:T(8,128)(2,1)} all-to-all(bf16[8,16,64,128]{3,2,1,0:T(8,128)(2,1)} %bitcast.85), channel_id=1, replica_groups=mesh['sub'=8,'rep'=4] {'sub'}, dimensions={0} | all-to-all | bytes 4194304 | tf_op jit(solution)/shard_map/all_to_all | solution.py:78
  154.5 3.3 %gather_fusion.1 = bf16[64,64,128]{2,1,0:T(8,128)(2,1)} fusion(bf16[8,16,64,128]{3,2,1,0:T(8,128)(2,1)} %all_to_all.27, s32[64]{0:T(128)S(1)} %bitcast.89), kind=kCustom, calls=%fused_computation.1 | custom fusion | bytes 2097664 | tf_op jit(solution)/shard_map/gather | solution.py:79
  157.8 9.1 %fusion.1 = bf16[8,8,8,8,128]{4,3,2,1,0:T(8,128)(2,1)S(1)} fusion(bf16[8,1024,1024]{2,1,0:T(8,128)(2,1)} %param.8, bf16[8,8,8,8,128]{4,3,2,1,0:T(8,128)(2,1)} %bitcast.88), kind=kOutput, calls=%fused_computation.12 | convolution fusion | flops 1074266112 | bytes 18874368 | tf_op jit(solution)/shard_map/skl,slm->skm/dot_general | solution.py:10
  167.0 1.3 copy.52
  168.2 1.9 broadcast.81
  170.1 9.8 %scatter_fusion.3 = bf16[8,16,64,128]{3,2,1,0:T(8,128)(2,1)} fusion(bf16[8,16,64,128]{3,2,1,0:T(8,128)(2,1)} %broadcast.81, s32[64]{0:T(128)S(1)} %get-tuple-element.2, bf16[64,64,128]{2,1,0:T(8,128)(2,1)} %bitcast.86), kind=kCustom, calls=%fused_computation.5 | custom fusion | bytes 3146240 | tf_op jit(solution)/shard_map/scatter | solution.py:36
  179.9 30.1 %all_to_all.28 = bf16[8,16,64,128]{3,2,1,0:T(8,128)(2,1)S(1)} all-to-all(bf16[8,16,64,128]{3,2,1,0:T(8,128)(2,1)} %scatter_fusion.3), channel_id=1, replica_groups=mesh['sub'=8,'rep'=4] {'sub'}, dimensions={0} | all-to-all | bytes 4194304 | tf_op jit(solution)/shard_map/all_to_all | solution.py:82
  210.0 2.5 %bitcast_convert_fusion = f32[128,64,128]{2,1,0:T(8,128)} fusion(bf16[8,16,64,128]{3,2,1,0:T(8,128)(2,1)S(1)} %all_to_all.28), kind=kLoop, calls=%fused_computation.7 | loop fusion | flops 1048576 | bytes 6291456 | tf_op jit(solution)/shard_map/convert_element_type | solution.py:41
  212.6 13.6 %scatter_fusion.4 = f32[16,64,128]{2,1,0:T(8,128)S(1)} fusion(f32[16,64,128]{2,1,0:T(8,128)S(1)} %broadcast.74, s32[128]{0:T(128)S(1)} %fusion.14, f32[128,64,128]{2,1,0:T(8,128)} %bitcast_convert_fusion), kind=kCustom, calls=%fused_computation.6 | custom fusion | flops 1048576 | bytes 12583424 | tf_op jit(solution)/shard_map/scatter-add | solution.py:42
  (19 shorter events, 3.9 us)
Async XLA Ops:
  0.6 115.0 %copy-start = (bf16[1024,1024]{1,0:T(8,128)(2,1)S(1)}, bf16[1024,1024]{1,0:T(8,128)(2,1)}, u32[]{:S(2)}) copy-start(bf16[1024,1024]{1,0:T(8,128)(2,1)} %param.13) | copy-start | bytes 6291460
  13.1 25.4 %all-to-all-start = ((s32[8,1,16]{2,1,0:T(1,128)}), s32[8,1,16]{2,1,0:T(1,128)S(1)}, u32[]{:S(2)}, u32[]{:S(2)}) async-start(s32[8,1,16]{2,1,0:T(1,128)} %bitcast.4), calls=%async_computation | async-start | bytes 8192 | tf_op jit(solution)/shard_map/all_to_all | solution.py:64
  38.5 4.5 %copy-start.1 = (s32[2048]{0:T(1024)S(1)}, s32[2048]{0:T(1024)}, u32[]{:S(2)}) copy-start(s32[2048]{0:T(1024)} %param.11) | copy-start | bytes 24580
  38.5 31.1 %all-to-all-start.1 = ((bf16[8,16,64,128]{3,2,1,0:T(8,128)(2,1)}), bf16[8,16,64,128]{3,2,1,0:T(8,128)(2,1)}, u32[]{:S(2)}, u32[]{:S(2)}) async-start(bf16[8,16,64,128]{3,2,1,0:T(8,128)(2,1)} %scatter_fusion.1), calls=%async_computation.1 | async-start | bytes 4194304 | tf_op jit(solution)/shard_map/all_to_all | solution.py:63
where the time goes:
time: 229 us; the launch traced here: 227 us
  blocking collectives  86.3 us (38%)
  local copies, waits for them, and re-layouts  41 us (18%)
  other arithmetic  38 us (17%)
  matrix products  26 us (11%)
  waiting for transfers between devices  25.3 us (11%)
  starting transfers between devices  9.66 us (4%)
    all_to_all x1, blocking collectives, per_device(): lax.all_to_all(requested, 'sub', split_axis=0, concat_axis=0, tiled=True)  30.9 us
    all_to_all x1, blocking collectives, per_device(): lax.all_to_all(pack_slots(make_blocks(again, width), dests, ranks, peers,...  30.1 us
    scatter-add x2, other arithmetic, accumulate(): jnp.zeros((own_blocks, columns, width), jnp.float32).at[got_ids.reshape(-1)]  27.2 us
    psum x1, blocking collectives, per_device(): summed = lax.psum(coeff, 'sub')  25.4 us
    all_to_all x1, waiting for transfers between devices, per_device(): lax.all_to_all(packed, 'sub', split_axis=0, concat_axis=0, tiled=True)  25.3 us
    scatter x2, local copies, waits for them, and re-layouts, pack_slots(): jnp.zeros((peers, slots, columns, width), jnp.bfloat16).at[dests, ranks]  18.7 us
    dot_general x2, matrix products, apply_local(): jnp.einsum('skl,slm->skm', inputs, operators, preferred_element_type=jnp....  18.2 us
    scatter x1, local copies, waits for them, and re-layouts, per_device(): jnp.zeros((peers, slots), jnp.int32).at[dests, ranks].set(dual_block)  10.2 us
  transfers between devices with their start and end apart: 2, of which 1 were waited for; matrix products, arithmetic and copies ran while one was open for 9% of the time, Pallas kernels for 0%

commit v1 on v0

v1 whole, which is shorter than its diff:
```python
import functools

import jax
import jax.numpy as jnp
from jax import lax
from jax.experimental import pallas as pl
from jax.experimental.pallas import tpu as pltpu
from jax.sharding import PartitionSpec as P

BLK = 128
FLOWS = 4
MESH = pl.DeviceIdType.MESH
VMEM_LIMIT = 62 * 1024 * 1024


def add_terms(owner_ref, block_ref, s, prod, acc, per_sub, own_blocks):
    for j in range(per_sub):
        row = s * per_sub + j
        g = owner_ref[row] * own_blocks + block_ref[row]
        acc[g] += prod[:, j * BLK : (j + 1) * BLK]


def first_kernel(own_blocks, owner_ref, block_ref, loads_ref, op_ref, out_ref, acc):
    s = pl.program_id(0)

    @pl.when(s == 0)
    def _():
        acc[...] = jnp.zeros_like(acc)

    prod = jnp.dot(loads_ref[0], op_ref[0], preferred_element_type=jnp.float32)
    add_terms(owner_ref, block_ref, s, prod, acc, op_ref.shape[2] // BLK, own_blocks)

    @pl.when(s == pl.num_programs(0) - 1)
    def _():
        out_ref[...] = acc[...].astype(jnp.bfloat16)


def second_kernel(own_blocks, owner_ref, block_ref, all_ref, op_ref, out_ref, acc):
    s = pl.program_id(0)
    per_sub = op_ref.shape[2] // BLK

    @pl.when(s == 0)
    def _():
        acc[...] = jnp.zeros_like(acc)

    picked = []
    for j in range(per_sub):
        row = s * per_sub + j
        picked.append(all_ref[owner_ref[row] * own_blocks + block_ref[row]])
    local = jnp.concatenate(picked, axis=1)
    prod = jnp.dot(local, op_ref[0], preferred_element_type=jnp.float32)
    add_terms(owner_ref, block_ref, s, prod, acc, per_sub, own_blocks)

    @pl.when(s == pl.num_programs(0) - 1)
    def _():
        out_ref[...] = acc[...].astype(jnp.bfloat16)


def local_call(kernel, name, owner, block, x, x_spec, operators, duals, own_blocks, columns):
    subs, rows, _ = operators.shape
    return pl.pallas_call(
        functools.partial(kernel, own_blocks),
        out_shape=jax.ShapeDtypeStruct((duals, columns, BLK), jnp.bfloat16),
        grid_spec=pltpu.PrefetchScalarGridSpec(
            num_scalar_prefetch=2,
            grid=(subs,),
            in_specs=[x_spec, pl.BlockSpec((1, rows, rows), lambda s, *_: (s, 0, 0))],
            out_specs=pl.BlockSpec((duals, columns, BLK), lambda s, *_: (0, 0, 0)),
            scratch_shapes=[pltpu.VMEM((duals, columns, BLK), jnp.float32)],
        ),
        compiler_params=pltpu.CompilerParams(
            dimension_semantics=("arbitrary",), vmem_limit_bytes=VMEM_LIMIT
        ),
        name=name,
    )(owner, block, x, operators)


def flip(me, r, bits):
    out = me
    for b in range(bits):
        if (r >> b) & 1:
            out = out + (1 - 2 * (me // (1 << b) % 2)) * (1 << b)
    return out


def plan(bits, flows):
    rest = list(range(1, bits))
    return [[0] + (rest if f % 2 == 0 else rest[::-1]) for f in range(flows)]


def step_of(r, order):
    for t, b in enumerate(order):
        if (r >> b) & 1:
            return t
    return len(order)


def slot_table(n, order):
    table, done = {}, 0
    for t, b in enumerate(order):
        done |= 1 << b
        for r in range(n):
            if r & done == 0:
                table[(t, r)] = len(table)
    return table


def entry_barrier(me, peers, bits):
    barrier = pltpu.get_barrier_semaphore()
    for r in peers:
        pl.semaphore_signal(
            barrier, inc=1, device_id={"sub": flip(me, r, bits)}, device_id_type=MESH
        )
    pl.semaphore_wait(barrier, len(peers))


def reduce_scatter(n, bits, me, dense, stage, recv, send_sem, recv_sem, per):
    orders = plan(bits, FLOWS)
    tables = [slot_table(n, order) for order in orders]
    sends = []

    def copy_of(f, r, t, src):
        b = orders[f][t]
        slot = tables[f][(t, r ^ (1 << b))]
        return pltpu.make_async_remote_copy(
            src_ref=src,
            dst_ref=recv.at[f, slot],
            send_sem=send_sem.at[f, slot],
            recv_sem=recv_sem.at[f, slot],
            device_id={"sub": flip(me, 1 << b, bits)},
            device_id_type=MESH,
        )

    def total(f, r, steps):
        part = dense[flip(me, r, bits), pl.ds(f * per, per)].astype(jnp.float32)
        for t in range(steps):
            slot = tables[f][(t, r)]
            pltpu.make_async_remote_copy(
                src_ref=recv.at[f, slot],
                dst_ref=recv.at[f, slot],
                send_sem=send_sem.at[f, slot],
                recv_sem=recv_sem.at[f, slot],
                device_id={"sub": flip(me, 1, bits)},
                device_id_type=MESH,
            ).wait_recv()
            part = part + recv[f, slot].astype(jnp.float32)
        return part

    for t in range(bits):
        for f in range(FLOWS):
            b = orders[f][t]
            group = [r for r in range(n) if step_of(r, orders[f]) == t]
            group.sort(key=lambda r: step_of(r ^ (1 << b), orders[f]))
            for r in group:
                if t == 0:
                    src = dense.at[flip(me, r, bits), pl.ds(f * per, per)]
                else:
                    src = stage.at[f, r]
                    stage[f, r] = total(f, r, t).astype(jnp.bfloat16)
                copy = copy_of(f, r, t, src)
                copy.start()
                sends.append(copy)
    return [total(f, 0, bits) for f in range(FLOWS)], sends


def middle_kernel(
    n,
    dense,
    scale,
    basis,
    coarse,
    start_ref,
    dual_ref,
    gat,
    stage,
    recv,
    cpart,
    cgot,
    call,
    dualb,
    send_sem,
    recv_sem,
    csend_sem,
    crecv_sem,
    dsend_sem,
    drecv_sem,
    gsend_sem,
    grecv_sem,
):
    bits = n.bit_length() - 1
    me = lax.axis_index("sub")
    own_blocks, columns = (dense.shape[1], dense.shape[2])
    per = own_blocks // FLOWS
    entry_barrier(me, list(range(1, n)), bits)
    totals, sends = reduce_scatter(
        n, bits, me, dense, stage, recv, send_sem, recv_sem, per
    )
    weight = 1.0 / (1.0 + scale[...].astype(jnp.float32))
    for f in range(FLOWS):
        for i in range(per):
            blk = f * per + i
            part = totals[f][i] * weight[blk : blk + 1, :]
            dual_ref[:, blk * BLK : (blk + 1) * BLK] = part
            dualb[:, blk * BLK : (blk + 1) * BLK] = part.astype(jnp.bfloat16)
    coeff = jnp.dot(dualb[...], basis[...], preferred_element_type=jnp.float32)

    groups, width = (call.shape[0], call.shape[2])
    rows = n // groups
    tall = columns // rows

    def piece(ref, p):
        return ref.at[p // rows, pl.ds(pl.multiple_of(p % rows * tall, tall), tall)]

    for c in range(groups):
        cpart[c] = coeff[:, c * width : (c + 1) * width].astype(jnp.bfloat16)
    out = []
    for r in range(1, n):
        peer = flip(me, r, bits)
        copy = pltpu.make_async_remote_copy(
            src_ref=piece(cpart, peer),
            dst_ref=cgot.at[r],
            send_sem=csend_sem.at[r],
            recv_sem=crecv_sem.at[r],
            device_id={"sub": peer},
            device_id_type=MESH,
        )
        copy.start()
        out.append(copy)
    mine = piece(cpart, me)[...].astype(jnp.float32)
    for r, copy in zip(range(1, n), out):
        copy.wait_recv()
        mine = mine + cgot[r].astype(jnp.float32)
    piece(call, me)[...] = mine.astype(jnp.bfloat16)
    back = []
    for r in range(1, n):
        copy = pltpu.make_async_remote_copy(
            src_ref=piece(call, me),
            dst_ref=piece(call, me),
            send_sem=dsend_sem.at[r],
            recv_sem=drecv_sem.at[r],
            device_id={"sub": flip(me, r, bits)},
            device_id_type=MESH,
        )
        copy.start()
        back.append(copy)
    for copy in back:
        copy.wait_recv()
    solved = jnp.dot(call[0], coarse[0:width], preferred_element_type=jnp.float32)
    for c in range(1, groups):
        solved = solved + jnp.dot(
            call[c], coarse[c * width : (c + 1) * width], preferred_element_type=jnp.float32
        )
    solved = solved.astype(jnp.bfloat16)
    orders = [order[::-1] for order in plan(bits, FLOWS)]

    def gather_copy(f, r, b):
        where = gat.at[flip(me, r, bits), pl.ds(f * per, per)]
        land = r ^ (1 << b)
        return pltpu.make_async_remote_copy(
            src_ref=where,
            dst_ref=where,
            send_sem=gsend_sem.at[f, land],
            recv_sem=grecv_sem.at[f, land],
            device_id={"sub": flip(me, 1 << b, bits)},
            device_id_type=MESH,
        )

    def arrived(f, r):
        where = gat.at[flip(me, r, bits), pl.ds(f * per, per)]
        pltpu.make_async_remote_copy(
            src_ref=where,
            dst_ref=where,
            send_sem=gsend_sem.at[f, r],
            recv_sem=grecv_sem.at[f, r],
            device_id={"sub": flip(me, 1, bits)},
            device_id_type=MESH,
        ).wait_recv()

    for f in range(FLOWS):
        span = slice(f * per * BLK, (f + 1) * per * BLK)
        part = lax.dot_general(
            solved, basis[span], (((1,), (1,)), ((), ())), preferred_element_type=jnp.float32
        )
        start_ref[:, span] = part
        for i in range(per):
            gat[me, f * per + i] = part[:, i * BLK : (i + 1) * BLK].astype(jnp.bfloat16)
        for b in orders[f]:
            copy = gather_copy(f, 0, b)
            copy.start()
            sends.append(copy)
    known = [[] for _ in range(FLOWS)]
    for u in range(bits):
        for f in range(FLOWS):
            b = orders[f][u]
            if u > 0:
                last = 1 << orders[f][u - 1]
                fresh = [last] + [r ^ last for r in known[f]]
                for r in fresh:
                    arrived(f, r)
                known[f] = known[f] + fresh
                for r in known[f]:
                    copy = gather_copy(f, r, b)
                    copy.start()
                    sends.append(copy)
    for f in range(FLOWS):
        last = 1 << orders[f][bits - 1]
        for r in [last] + [r ^ last for r in known[f]]:
            arrived(f, r)
    for copy in sends + out + back:
        copy.wait_send()


def last_kernel(n, dense, scale, dual_ref, resid_ref, stage, recv, send_sem, recv_sem):
    bits = n.bit_length() - 1
    me = lax.axis_index("sub")
    own_blocks = dense.shape[1]
    per = own_blocks // FLOWS
    entry_barrier(me, [1 << b for b in range(bits)], bits)
    totals, sends = reduce_scatter(
        n, bits, me, dense, stage, recv, send_sem, recv_sem, per
    )
    weight = 1.0 / (1.0 + scale[...].astype(jnp.float32))
    for f in range(FLOWS):
        for i in range(per):
            blk = f * per + i
            span = slice(blk * BLK, (blk + 1) * BLK)
            resid_ref[:, span] = dual_ref[:, span] - totals[f][i] * weight[blk : blk + 1, :]
    for copy in sends:
        copy.wait_send()


def per_device(n, loads, operators, owner, dual_block, scale_index, basis, coarse):
    columns = loads.shape[1]
    local_rows = basis.shape[0]
    own_blocks = local_rows // BLK
    duals = n * own_blocks
    owner = owner.reshape(-1)
    scale = scale_index.reshape(own_blocks, BLK)
    per = own_blocks // FLOWS
    dirs = coarse.shape[0]
    vmem = pl.BlockSpec(memory_space=pltpu.VMEM)
    dma = pltpu.SemaphoreType.DMA

    partial = local_call(
        first_kernel,
        "first_local",
        owner,
        dual_block,
        loads,
        pl.BlockSpec((1, columns, loads.shape[2]), lambda s, *_: (s, 0, 0)),
        operators,
        duals,
        own_blocks,
        columns,
    )
    rows = min(n, columns // 16)
    groups = n // rows
    comm = [
        pltpu.VMEM((FLOWS, n, per, columns, BLK), jnp.bfloat16),
        pltpu.VMEM((FLOWS, n - 1, per, columns, BLK), jnp.bfloat16),
    ]
    start, dual, everywhere = pl.pallas_call(
        functools.partial(middle_kernel, n),
        out_shape=(
            jax.ShapeDtypeStruct((columns, local_rows), jnp.float32),
            jax.ShapeDtypeStruct((columns, local_rows), jnp.float32),
            jax.ShapeDtypeStruct((n, own_blocks, columns, BLK), jnp.bfloat16),
        ),
        in_specs=[vmem] * 4,
        out_specs=(vmem, vmem, vmem),
        scratch_shapes=comm
        + [
            pltpu.VMEM((groups, columns, dirs // groups), jnp.bfloat16),
            pltpu.VMEM((n, columns // rows, dirs // groups), jnp.bfloat16),
            pltpu.VMEM((groups, columns, dirs // groups), jnp.bfloat16),
            pltpu.VMEM((columns, local_rows), jnp.bfloat16),
            dma((FLOWS, n - 1)),
            dma((FLOWS, n - 1)),
            dma((n,)),
            dma((n,)),
            dma((n,)),
            dma((n,)),
            dma((FLOWS, n)),
            dma((FLOWS, n)),
        ],
        compiler_params=pltpu.CompilerParams(
            collective_id=0, has_side_effects=True, vmem_limit_bytes=VMEM_LIMIT
        ),
        name="middle",
    )(partial.reshape(n, own_blocks, columns, BLK), scale, basis, coarse)
    again = local_call(
        second_kernel,
        "second_local",
        owner,
        dual_block,
        everywhere.reshape(duals, columns, BLK),
        pl.BlockSpec(
            (duals, columns, BLK), lambda s, *_: (0, 0, 0), pipeline_mode=pl.Buffered(1)
        ),
        operators,
        duals,
        own_blocks,
        columns,
    )
    resid = pl.pallas_call(
        functools.partial(last_kernel, n),
        out_shape=jax.ShapeDtypeStruct((columns, local_rows), jnp.float32),
        in_specs=[vmem] * 3,
        out_specs=vmem,
        scratch_shapes=comm + [dma((FLOWS, n - 1)), dma((FLOWS, n - 1))],
        compiler_params=pltpu.CompilerParams(
            collective_id=1, has_side_effects=True, vmem_limit_bytes=VMEM_LIMIT
        ),
        name="last",
    )(again.reshape(n, own_blocks, columns, BLK), scale, dual)
    return (start, resid)


def solution(mesh):
    return jax.shard_map(
        functools.partial(per_device, mesh.shape["sub"]),
        mesh=mesh,
        in_specs=(
            P("sub", "rep", None),
            P("sub", None, None),
            P("sub", None),
            P("sub"),
            P("sub"),
            P("sub", None),
            P(),
        ),
        out_specs=(P("rep", "sub"), P("rep", "sub")),
        check_vma=False,
    )
```

time: 229 us -> 87.9 us (0.38)
  blocking collectives: 86.3 us -> 0 us
  Pallas kernels: 0 us -> 84.3 us
  local copies, waits for them, and re-layouts: 41 us -> 2.67 us
  other arithmetic: 38 us -> 0 us
  matrix products: 26 us -> 0 us
  waiting for transfers between devices: 25.3 us -> 0 us
  starting transfers between devices: 9.66 us -> 0 us
    pallas_call x0 -> x4, Pallas kernels: none -> 84.3 us  [the longest x1 43.4 us: per_device(): pl.pallas_call(functools.partial(middle_kernel, n), out_shape=(jax.ShapeD...]
    all_to_all x2 -> x0, blocking collectives: 61 us -> none  [the longest x1 30.9 us: per_device(): lax.all_to_all(requested, 'sub', split_axis=0, concat_axis=0, tiled=True)]
    scatter x3 -> x0, local copies, waits for them, and re-layouts: 28.9 us -> none  [the longest x2 18.7 us: pack_slots(): jnp.zeros((peers, slots, columns, width), jnp.bfloat16).at[dests, ranks]]
    scatter-add x2 -> x0, other arithmetic: 27.2 us -> none  [accumulate(): jnp.zeros((own_blocks, columns, width), jnp.float32).at[got_ids.reshape(-1)]]
    dot_general x4 -> x0, matrix products: 26 us -> none  [the longest x2 18.2 us: apply_local(): jnp.einsum('skl,slm->skm', inputs, operators, preferred_element_type=jnp....]
    psum x1 -> x0, blocking collectives: 25.4 us -> none  [per_device(): summed = lax.psum(coeff, 'sub')]
    all_to_all x2 -> x0, waiting for transfers between devices: 25.3 us -> none  [the longest x1 25.3 us: per_device(): lax.all_to_all(packed, 'sub', split_axis=0, concat_axis=0, tiled=True)]
    all_to_all x2 -> x0, starting transfers between devices: 9.66 us -> none  [the longest x1 5.2 us: per_device(): lax.all_to_all(id_slots, 'sub', split_axis=0, concat_axis=0, tiled=True)]
  transfers between devices with their start and end apart: 2 -> 0, of which waited for: 1 -> 0; matrix products, arithmetic and copies ran while one was open for 9% -> 0% of each run, Pallas kernels for 0% -> 0%
where the time goes in v1:
time: 87.9 us; the launch traced here: 87.6 us
  Pallas kernels  84.3 us (96%)
  local copies, waits for them, and re-layouts  2.67 us (3%)
    pallas_call x1, Pallas kernels, per_device(): pl.pallas_call(functools.partial(middle_kernel, n), out_shape=(jax.ShapeD...  43.4 us
    pallas_call x2, Pallas kernels, local_call(): pl.pallas_call(functools.partial(kernel, own_blocks), out_shape=jax.Shape...  24.7 us
    pallas_call x1, Pallas kernels, per_device(): pl.pallas_call(functools.partial(last_kernel, n), out_shape=jax.ShapeDtyp...  16.2 us
    unnamed x4, local copies, waits for them, and re-layouts  2.67 us

profile of v1, /device:TPU:0, one launch (start us, length us, event | category | flops | bytes accessed | tf_op | source)
XLA Modules:
  0.0 87.6 jit_solution(4720185420656551536)
XLA Ops:
  0.6 12.2 %first_local.1 = bf16[128,64,128]{2,1,0:T(8,128)(2,1)} custom-call(s32[64]{0:T(128)} %bitcast.10, s32[64]{0:T(128)} %block_ref.3, bf16[8,64,1024]{2,1,0:T(8,128)(2,1)} %loads_ref.1, bf16[8,1024,1024]{2,1,0:T(8,128)(2,1)} %op_ref.3), custom_call_target="tpu_custom_call" | custom-call | tf_op jit(solution)/shard_map/first_local/pallas_call | solution.py:61
  12.8 43.4 %middle.1 = (f32[64,2048]{1,0:T(8,128)}, f32[64,2048]{1,0:T(8,128)}, bf16[8,16,64,128]{3,2,1,0:T(8,128)(2,1)}) custom-call(bf16[8,16,64,128]{3,2,1,0:T(8,128)(2,1)} %bitcast.5, s32[16,128]{1,0:T(8,128)} %bitcast.8, bf16[2048,1024]{1,0:T(8,128)(2,1)} %basis.1, bf16[1024,1024]{1,0:T(8,128)(2,1)} %coarse.1), custom_call_target="tpu_custom_call" | custom-call | tf_op jit(solution)/shard_map/middle/pallas_call | solution.py:362
  56.2 12.5 %second_local.1 = bf16[128,64,128]{2,1,0:T(8,128)(2,1)} custom-call(s32[64]{0:T(128)} %bitcast.11, s32[64]{0:T(128)} %block_ref.3, bf16[128,64,128]{2,1,0:T(8,128)(2,1)} %bitcast.7, bf16[8,1024,1024]{2,1,0:T(8,128)(2,1)} %op_ref.3), custom_call_target="tpu_custom_call" | custom-call | tf_op jit(solution)/shard_map/second_local/pallas_call | solution.py:61
  68.7 0.0 copy-start
  68.7 16.2 %last.1 = f32[64,2048]{1,0:T(8,128)} custom-call(bf16[8,16,64,128]{3,2,1,0:T(8,128)(2,1)} %bitcast.6, s32[16,128]{1,0:T(8,128)} %bitcast.9, f32[64,2048]{1,0:T(8,128)} %get-tuple-element.7.dual_ref), custom_call_target="tpu_custom_call" | custom-call | tf_op jit(solution)/shard_map/last/pallas_call | solution.py:405
  84.9 0.0 copy-done
  84.9 0.8 copy.11
  85.7 1.9 %copy.12 = f32[64,2048]{1,0:T(8,128)} copy(f32[64,2048]{1,0:T(8,128)} %last.1) | data formatting | bytes 1048576
Async XLA Ops:
  68.7 16.2 %copy-start = (f32[64,2048]{1,0:T(8,128)S(1)}, f32[64,2048]{1,0:T(8,128)}, u32[]{:S(2)}) copy-start(f32[64,2048]{1,0:T(8,128)} %get-tuple-element.10) | copy-start | bytes 1572868

commit v2 on v1

v2 whole, which is shorter than its diff:
```python
import functools

import jax
import jax.numpy as jnp
from jax import lax
from jax.experimental import pallas as pl
from jax.experimental.pallas import tpu as pltpu
from jax.sharding import PartitionSpec as P

BLK = 128
FLOWS = 4
MESH = pl.DeviceIdType.MESH
VMEM_LIMIT = 62 * 1024 * 1024
F32 = jnp.float32
BF16 = jnp.bfloat16


def flip(me, r, bits):
    out = me
    for b in range(bits):
        if (r >> b) & 1:
            out = out + (1 - 2 * (me // (1 << b) % 2)) * (1 << b)
    return out


def plan(bits, flows):
    rest = list(range(1, bits))
    return [[0] + (rest if f % 2 == 0 else rest[::-1]) for f in range(flows)]


def step_of(r, order):
    for t, b in enumerate(order):
        if (r >> b) & 1:
            return t
    return len(order)


def slot_table(n, order):
    table, done = {}, 0
    for t, b in enumerate(order):
        done |= 1 << b
        for r in range(n):
            if r & done == 0:
                table[(t, r)] = len(table)
    return table


def reduce_scatter(n, bits, me, local, stage, recv, send_sem, recv_sem):
    orders = plan(bits, FLOWS)
    tables = [slot_table(n, order) for order in orders]
    sends = []

    def copy_of(f, slot, src, b):
        return pltpu.make_async_remote_copy(
            src_ref=src,
            dst_ref=recv.at[f, slot],
            send_sem=send_sem.at[f, slot],
            recv_sem=recv_sem.at[f, slot],
            device_id={"sub": flip(me, 1 << b, bits)},
            device_id_type=MESH,
        )

    def total(f, r, steps):
        part = local(f, flip(me, r, bits))
        for t in range(steps):
            slot = tables[f][(t, r)]
            copy_of(f, slot, recv.at[f, slot], orders[f][t]).wait_recv()
            part = part + recv[f, slot].astype(F32)
        return part

    for t in range(bits):
        group = []
        for f in range(FLOWS):
            for r in range(n):
                if step_of(r, orders[f]) == t:
                    land = r ^ (1 << orders[f][t])
                    group.append((step_of(land, orders[f]), f, r, land))
        for _, f, r, land in sorted(group):
            stage[f, r - 1] = total(f, r, t).astype(BF16)
            copy = copy_of(f, tables[f][(t, land)], stage.at[f, r - 1], orders[f][t])
            copy.start()
            sends.append(copy)
    return sends, lambda f: total(f, 0, bits)


def kernel(
    n,
    target,
    links,
    scale,
    loads_hbm,
    operators_hbm,
    basis_hbm,
    coarse_hbm,
    start_ref,
    resid_ref,
    loads,
    operators,
    basis,
    coarse,
    runs,
    gat,
    stage,
    recv,
    cacc,
    cpart,
    cgot,
    call,
    dual,
    in_sem,
    op_sem,
    send_sem,
    recv_sem,
    csend_sem,
    crecv_sem,
    dsend_sem,
    drecv_sem,
    gsend_sem,
    grecv_sem,
):
    bits = n.bit_length() - 1
    me = lax.axis_index("sub")
    subs, columns, rows_in = loads.shape
    per_sub = rows_in // BLK
    nblocks = subs * per_sub
    own_blocks = gat.shape[0] // n
    per = own_blocks // FLOWS

    barrier = pltpu.get_barrier_semaphore()
    for r in range(1, n):
        pl.semaphore_signal(
            barrier, inc=1, device_id={"sub": flip(me, r, bits)}, device_id_type=MESH
        )
    load_copy = pltpu.make_async_copy(loads_hbm, loads, in_sem.at[0])
    basis_copy = pltpu.make_async_copy(basis_hbm, basis, in_sem.at[1])
    coarse_copy = pltpu.make_async_copy(coarse_hbm, coarse, in_sem.at[2])

    def op_copy(s):
        return pltpu.make_async_copy(operators_hbm.at[s], operators.at[s], op_sem.at[s])

    load_copy.start()
    for s in range(subs):
        op_copy(s).start()
    basis_copy.start()
    coarse_copy.start()
    runs[nblocks] = jnp.zeros((columns, BLK), F32)
    weight = 1.0 / (1.0 + scale[...].astype(F32))
    load_copy.wait()

    def add_runs(s, prod):
        for j in range(per_sub):
            row = s * per_sub + j
            term = prod[:, j * BLK : (j + 1) * BLK].astype(BF16).astype(F32)
            runs[row] = term + runs[links[row]]

    def first(s, carry):
        op_copy(s).wait()
        add_runs(s, jnp.dot(loads[s], operators[s], preferred_element_type=F32))
        return carry

    lax.fori_loop(0, subs, first, 0)

    def local(f, owner):
        base = nblocks + owner * own_blocks + f * per
        return jnp.stack([runs[links[base + i]] for i in range(per)])

    pl.semaphore_wait(barrier, n - 1)
    sends, finish = reduce_scatter(n, bits, me, local, stage, recv, send_sem, recv_sem)
    basis_copy.wait()
    coarse_copy.wait()
    for f in range(FLOWS):
        span = slice(f * per * BLK, (f + 1) * per * BLK)
        part = finish(f)
        pieces = []
        for i in range(per):
            blk = f * per + i
            pieces.append(part[i] * weight[blk : blk + 1, :])
        wide = jnp.concatenate(pieces, axis=1)
        dual[:, span] = wide
        coeff = jnp.dot(wide.astype(BF16), basis[span], preferred_element_type=F32)
        if f == 0:
            cacc[...] = coeff
        else:
            cacc[...] += coeff

    groups, width = (call.shape[0], call.shape[2])
    rows = n // groups
    tall = columns // rows

    def piece(ref, p):
        return ref.at[p // rows, pl.ds(pl.multiple_of(p % rows * tall, tall), tall)]

    for c in range(groups):
        cpart[c] = cacc[:, c * width : (c + 1) * width].astype(BF16)
    out = []
    for r in range(1, n):
        peer = flip(me, r, bits)
        copy = pltpu.make_async_remote_copy(
            src_ref=piece(cpart, peer),
            dst_ref=cgot.at[r],
            send_sem=csend_sem.at[r],
            recv_sem=crecv_sem.at[r],
            device_id={"sub": peer},
            device_id_type=MESH,
        )
        copy.start()
        out.append(copy)
    mine = piece(cpart, me)[...].astype(F32)
    for r, copy in zip(range(1, n), out):
        copy.wait_recv()
        mine = mine + cgot[r].astype(F32)
    piece(call, me)[...] = mine.astype(BF16)
    back = []
    for r in range(1, n):
        copy = pltpu.make_async_remote_copy(
            src_ref=piece(call, me),
            dst_ref=piece(call, me),
            send_sem=dsend_sem.at[r],
            recv_sem=drecv_sem.at[r],
            device_id={"sub": flip(me, r, bits)},
            device_id_type=MESH,
        )
        copy.start()
        back.append(copy)
    for r, copy in zip(range(1, n), back):
        there = piece(call, flip(me, r, bits))
        pltpu.make_async_remote_copy(
            src_ref=there,
            dst_ref=there,
            send_sem=dsend_sem.at[r],
            recv_sem=drecv_sem.at[r],
            device_id={"sub": flip(me, r, bits)},
            device_id_type=MESH,
        ).wait_recv()
    solved = jnp.dot(call[0], coarse[0:width], preferred_element_type=F32)
    for c in range(1, groups):
        solved = solved + jnp.dot(
            call[c], coarse[c * width : (c + 1) * width], preferred_element_type=F32
        )
    solved = solved.astype(BF16)
    orders = [order[::-1] for order in plan(bits, FLOWS)]

    def gather_copy(f, r, b):
        where = gat.at[pl.ds(flip(me, r, bits) * own_blocks + f * per, per)]
        land = r ^ (1 << b)
        return pltpu.make_async_remote_copy(
            src_ref=where,
            dst_ref=where,
            send_sem=gsend_sem.at[f, land],
            recv_sem=grecv_sem.at[f, land],
            device_id={"sub": flip(me, 1 << b, bits)},
            device_id_type=MESH,
        )

    def arrived(f, r):
        where = gat.at[pl.ds(flip(me, r, bits) * own_blocks + f * per, per)]
        pltpu.make_async_remote_copy(
            src_ref=where,
            dst_ref=where,
            send_sem=gsend_sem.at[f, r],
            recv_sem=grecv_sem.at[f, r],
            device_id={"sub": flip(me, 1, bits)},
            device_id_type=MESH,
        ).wait_recv()

    gathers = []
    for f in range(FLOWS):
        span = slice(f * per * BLK, (f + 1) * per * BLK)
        part = lax.dot_general(
            solved, basis[span], (((1,), (1,)), ((), ())), preferred_element_type=F32
        )
        start_ref[:, span] = part
        for i in range(per):
            gat[me * own_blocks + f * per + i] = part[:, i * BLK : (i + 1) * BLK].astype(BF16)
        for b in orders[f]:
            copy = gather_copy(f, 0, b)
            copy.start()
            gathers.append(copy)
    known = [[] for _ in range(FLOWS)]
    for u in range(bits):
        for f in range(FLOWS):
            b = orders[f][u]
            if u > 0:
                last = 1 << orders[f][u - 1]
                fresh = [last] + [r ^ last for r in known[f]]
                for r in fresh:
                    arrived(f, r)
                known[f] = known[f] + fresh
                for r in known[f]:
                    copy = gather_copy(f, r, b)
                    copy.start()
                    gathers.append(copy)
    for copy in sends + out + back:
        copy.wait_send()
    for f in range(FLOWS):
        last = 1 << orders[f][bits - 1]
        for r in [last] + [r ^ last for r in known[f]]:
            arrived(f, r)

    def second(s, carry):
        picked = [gat[target[s * per_sub + j]] for j in range(per_sub)]
        held = jnp.concatenate(picked, axis=1)
        add_runs(s, jnp.dot(held, operators[s], preferred_element_type=F32))
        return carry

    lax.fori_loop(0, subs, second, 0)
    sends, finish = reduce_scatter(n, bits, me, local, stage, recv, send_sem, recv_sem)
    for f in range(FLOWS):
        part = finish(f)
        for i in range(per):
            blk = f * per + i
            span = slice(blk * BLK, (blk + 1) * BLK)
            resid_ref[:, span] = dual[:, span] - part[i] * weight[blk : blk + 1, :]
    for copy in gathers + sends:
        copy.wait_send()


def per_device(n, loads, operators, owner, dual_block, scale_index, basis, coarse):
    subs, columns, rows_in = loads.shape
    local_rows = basis.shape[0]
    own_blocks = local_rows // BLK
    duals = n * own_blocks
    target = owner.reshape(-1) * own_blocks + dual_block
    nblocks = target.shape[0]
    key = jnp.concatenate([target, jnp.arange(duals, dtype=jnp.int32)])
    bound = jnp.minimum(jnp.arange(nblocks + duals, dtype=jnp.int32), nblocks)
    places = jnp.arange(nblocks, dtype=jnp.int32)
    hit = (key[:, None] == target[None, :]) & (places[None, :] < bound[:, None])
    found = jnp.max(jnp.where(hit, places[None, :], -1), axis=1)
    links = jnp.where(found < 0, nblocks, found)
    scale = scale_index.reshape(own_blocks, BLK)
    per = own_blocks // FLOWS
    dirs = coarse.shape[0]
    rows = min(n, columns // 16)
    groups = n // rows
    vmem = pl.BlockSpec(memory_space=pltpu.VMEM)
    smem = pl.BlockSpec(memory_space=pltpu.SMEM)
    hbm = pl.BlockSpec(memory_space=pl.ANY)
    dma = pltpu.SemaphoreType.DMA
    out = jax.ShapeDtypeStruct((columns, local_rows), F32)
    return pl.pallas_call(
        functools.partial(kernel, n),
        out_shape=(out, out),
        in_specs=[smem, smem, vmem] + [hbm] * 4,
        out_specs=(vmem, vmem),
        scratch_shapes=[
            pltpu.VMEM(loads.shape, BF16),
            pltpu.VMEM(operators.shape, BF16),
            pltpu.VMEM(basis.shape, BF16),
            pltpu.VMEM(coarse.shape, BF16),
            pltpu.VMEM((nblocks + 1, columns, BLK), F32),
            pltpu.VMEM((duals, columns, BLK), BF16),
            pltpu.VMEM((FLOWS, n - 1, per, columns, BLK), BF16),
            pltpu.VMEM((FLOWS, n - 1, per, columns, BLK), BF16),
            pltpu.VMEM((columns, dirs), F32),
            pltpu.VMEM((groups, columns, dirs // groups), BF16),
            pltpu.VMEM((n, columns // rows, dirs // groups), BF16),
            pltpu.VMEM((groups, columns, dirs // groups), BF16),
            pltpu.VMEM((columns, local_rows), F32),
            dma((3,)),
            dma((subs,)),
            dma((FLOWS, n - 1)),
            dma((FLOWS, n - 1)),
            dma((n,)),
            dma((n,)),
            dma((n,)),
            dma((n,)),
            dma((FLOWS, n)),
            dma((FLOWS, n)),
        ],
        compiler_params=pltpu.CompilerParams(
            collective_id=0, has_side_effects=True, vmem_limit_bytes=VMEM_LIMIT
        ),
        name="feti",
    )(target, links, scale, loads, operators, basis, coarse)


def solution(mesh):
    return jax.shard_map(
        functools.partial(per_device, mesh.shape["sub"]),
        mesh=mesh,
        in_specs=(
            P("sub", "rep", None),
            P("sub", None, None),
            P("sub", None),
            P("sub"),
            P("sub"),
            P("sub", None),
            P(),
        ),
        out_specs=(P("rep", "sub"), P("rep", "sub")),
        check_vma=False,
    )
```

time: 87.9 us -> 68 us (0.77)
  Pallas kernels: 84.3 us -> 62 us
  other arithmetic: 0 us -> 1.42 us
  local copies, waits for them, and re-layouts: 2.67 us -> 3.75 us
    pallas_call x4 -> x1, Pallas kernels: 84.3 us -> 62 us  [per_device(): pl.pallas_call(functools.partial(kernel, n), out_shape=(out, out), in_spe...]
    unnamed x4, local copies, waits for them, and re-layouts: 2.67 us -> 3.75 us
where the time goes in v2:
time: 68 us; the launch traced here: 67.8 us
  Pallas kernels  62 us (91%)
  local copies, waits for them, and re-layouts  3.75 us (6%)
  other arithmetic  1.42 us (2%)
    pallas_call x1, Pallas kernels, per_device(): pl.pallas_call(functools.partial(kernel, n), out_shape=(out, out), in_spe...  62 us
    unnamed x4, local copies, waits for them, and re-layouts  3.75 us

profile of v2, /device:TPU:0, one launch (start us, length us, event | category | flops | bytes accessed | tf_op | source)
XLA Modules:
  0.0 67.8 jit_solution(15727104313729303450)
XLA Ops:
  0.6 0.7 bitcast_add_fusion.target
  1.3 0.0 copy-start
  1.3 0.1 pad_add_fusion
  1.4 0.1 select_reduce_fusion
  1.5 0.6 compare_select_fusion.links
  2.1 0.0 copy-done
  2.1 62.0 %feti.1 = (f32[64,2048]{1,0:T(8,128)}, f32[64,2048]{1,0:T(8,128)}) custom-call(s32[64]{0:T(128)} %copy-done, s32[192]{0:T(256)} %compare_select_fusion.links, s32[16,128]{1,0:T(8,128)} %bitcast.3, bf16[8,64,1024]{2,1,0:T(8,128)(2,1)} %loads_hbm.1, bf16[8,1024,1024]{2,1,0:T(8,128)(2,1)} %operators_hbm.1, bf16[2048,1024]{1,0:T(8,128)(2,1)} %basis_hbm.1, ...), custom_call_target="tpu_custom_call" | custom-call | tf_op jit(solution)/shard_map/feti/pallas_call | solution.py:341
  64.0 1.9 %copy.11 = f32[64,2048]{1,0:T(8,128)} copy(f32[64,2048]{1,0:T(8,128)} %get-tuple-element.6) | data formatting | bytes 1048576
  65.9 1.9 %copy.12 = f32[64,2048]{1,0:T(8,128)} copy(f32[64,2048]{1,0:T(8,128)} %get-tuple-element.7) | data formatting | bytes 1048576
  (1 shorter events, 0.0 us)
Async XLA Ops:
  1.3 0.7 %copy-start = (s32[64]{0:T(128)}, s32[64]{0:T(128)S(1)}, u32[]{:S(2)}) copy-start(s32[64]{0:T(128)S(1)} %bitcast_add_fusion.target) | copy-start | bytes 772

commit v3 on v2

v3 whole, which is shorter than its diff:
```python
import functools

import jax
import jax.numpy as jnp
from jax import lax
from jax.experimental import pallas as pl
from jax.experimental.pallas import tpu as pltpu
from jax.sharding import PartitionSpec as P

BLK = 128
FLOWS = 2
GROUPS = 2
PARTS = 2
MESH = pl.DeviceIdType.MESH
VMEM_LIMIT = 62 * 1024 * 1024
F32 = jnp.float32
BF16 = jnp.bfloat16


def flip(me, r, bits):
    out = me
    for b in range(bits):
        if (r >> b) & 1:
            out = out + (1 - 2 * (me // (1 << b) % 2)) * (1 << b)
    return out


def plan(bits, flows):
    rest = list(range(1, bits))
    return [[0] + (rest if f % 2 == 0 else rest[::-1]) for f in range(flows)]


def step_of(r, order):
    for t, b in enumerate(order):
        if (r >> b) & 1:
            return t
    return len(order)


def slot_table(n, order):
    table, done = {}, 0
    for t, b in enumerate(order):
        done |= 1 << b
        for r in range(n):
            if r & done == 0:
                table[(t, r)] = len(table)
    return table


def interleave(pipelines):
    pipelines = list(pipelines)
    while pipelines:
        for one in list(pipelines):
            if next(one, "end") == "end":
                pipelines.remove(one)


def kernel(
    n,
    target,
    links,
    scale,
    loads_hbm,
    operators_hbm,
    basis_hbm,
    coarse_hbm,
    start_ref,
    resid_ref,
    loads,
    operators,
    basis,
    coarse,
    runs,
    gathered,
    stage,
    recv,
    cpart,
    cgot,
    call,
    dual,
    in_sem,
    op_sem,
    send_sem,
    recv_sem,
    csend_sem,
    crecv_sem,
    dsend_sem,
    drecv_sem,
    gsend_sem,
    grecv_sem,
):
    bits = n.bit_length() - 1
    me = lax.axis_index("sub")
    subs, columns, rows_in = loads.shape
    per_sub = rows_in // BLK
    nblocks = subs * per_sub
    own_blocks = gathered[0].shape[0] // n
    per = own_blocks // FLOWS
    height = columns // GROUPS
    orders = plan(bits, FLOWS)
    tables = [slot_table(n, order) for order in orders]
    tall, width = (call.shape[2], call.shape[3])
    across = coarse.shape[0] // width

    barrier = pltpu.get_barrier_semaphore()
    for r in range(1, n):
        pl.semaphore_signal(
            barrier, inc=1, device_id={"sub": flip(me, r, bits)}, device_id_type=MESH
        )
    load_copy = pltpu.make_async_copy(loads_hbm, loads, in_sem.at[0])
    basis_copy = pltpu.make_async_copy(basis_hbm, basis, in_sem.at[1])
    coarse_copy = pltpu.make_async_copy(coarse_hbm, coarse, in_sem.at[2])

    def op_copy(s):
        return pltpu.make_async_copy(operators_hbm.at[s], operators.at[s], op_sem.at[s])

    load_copy.start()
    for s in range(subs):
        op_copy(s).start()
    basis_copy.start()
    coarse_copy.start()
    runs[nblocks] = jnp.zeros((columns, BLK), F32)
    weight = 1.0 / (1.0 + scale[...].astype(F32))
    load_copy.wait()

    def add_runs(s, prod, lines):
        for j in range(per_sub):
            row = s * per_sub + j
            term = prod[:, j * BLK : (j + 1) * BLK].astype(BF16).astype(F32)
            runs[row, lines] = term + runs[links[row], lines]

    def first(s, carry):
        op_copy(s).wait()
        add_runs(s, jnp.dot(loads[s], operators[s], preferred_element_type=F32), slice(None))
        return carry

    lax.fori_loop(0, subs, first, 0)
    pl.semaphore_wait(barrier, n - 1)

    def remote(src, dst, sends, recvs, peer):
        return pltpu.make_async_remote_copy(
            src_ref=src,
            dst_ref=dst,
            send_sem=sends,
            recv_sem=recvs,
            device_id={"sub": peer},
            device_id_type=MESH,
        )

    def group(g):
        lines = slice(g * height, (g + 1) * height)
        gat = gathered[g]
        pending = []

        def go(copy):
            copy.start()
            pending.append(copy)

        def halve_copy(f, slot, src, b):
            return remote(
                src,
                recv.at[g, f, slot],
                send_sem.at[g, f, slot],
                recv_sem.at[g, f, slot],
                flip(me, 1 << b, bits),
            )

        def total(f, r, steps):
            base = nblocks + flip(me, r, bits) * own_blocks + f * per
            part = jnp.stack([runs[links[base + i], lines] for i in range(per)])
            for t in range(steps):
                slot = tables[f][(t, r)]
                halve_copy(f, slot, recv.at[g, f, slot], orders[f][t]).wait_recv()
                part = part + recv[g, f, slot].astype(F32)
            return part

        def halve_step(t):
            todo = []
            for f in range(FLOWS):
                for r in range(n):
                    if step_of(r, orders[f]) == t:
                        land = r ^ (1 << orders[f][t])
                        todo.append((step_of(land, orders[f]), f, r, land))
            for _, f, r, land in sorted(todo):
                stage[g, f, r - 1] = total(f, r, t).astype(BF16)
                go(halve_copy(f, tables[f][(t, land)], stage.at[g, f, r - 1], orders[f][t]))

        def settle():
            for copy in pending:
                copy.wait_send()
            pending.clear()

        for t in range(bits):
            halve_step(t)
            yield
        if g == 0:
            basis_copy.wait()
            coarse_copy.wait()
        wide = []
        for f in range(FLOWS):
            part = total(f, 0, bits)
            for i in range(per):
                blk = f * per + i
                wide.append(part[i] * weight[blk : blk + 1, :])
        wide = jnp.concatenate(wide, axis=1)
        dual[lines] = wide
        coeff = jnp.dot(wide.astype(BF16), basis[...], preferred_element_type=F32)
        for p in range(n):
            top, left = (p // across * tall, p % across * width)
            cpart[g, p] = coeff[top : top + tall, left : left + width].astype(BF16)
        for r in range(1, n):
            peer = flip(me, r, bits)
            go(
                remote(
                    cpart.at[g, peer],
                    cgot.at[g, r - 1],
                    csend_sem.at[g, r - 1],
                    crecv_sem.at[g, r - 1],
                    peer,
                )
            )
        yield
        mine = cpart[g, me].astype(F32)
        for r in range(1, n):
            here = cgot.at[g, r - 1]
            remote(
                here, here, csend_sem.at[g, r - 1], crecv_sem.at[g, r - 1], flip(me, r, bits)
            ).wait_recv()
            mine = mine + cgot[g, r - 1].astype(F32)
        call[g, me] = mine.astype(BF16)

        def spread_copy(r, p):
            there = call.at[g, p]
            return remote(
                there, there, dsend_sem.at[g, r - 1], drecv_sem.at[g, r - 1], flip(me, r, bits)
            )

        for r in range(1, n):
            go(spread_copy(r, me))
        yield
        for r in range(1, n):
            spread_copy(r, flip(me, r, bits)).wait_recv()
        bands = []
        for top in range(0, n, across):
            band = jnp.concatenate([call[g, top + c] for c in range(across)], axis=1)
            bands.append(band if n == across else band.astype(F32))
        whole = bands[0] if n == across else jnp.concatenate(bands, axis=0).astype(BF16)
        solved = jnp.dot(whole, coarse[...], preferred_element_type=F32).astype(BF16)

        def spot(f, r):
            return gat.at[pl.ds(flip(me, r, bits) * own_blocks + f * per, per)]

        def double_copy(f, r, b):
            land = r ^ (1 << b)
            return remote(
                spot(f, r),
                spot(f, r),
                gsend_sem.at[g, f, land - 1],
                grecv_sem.at[g, f, land - 1],
                flip(me, 1 << b, bits),
            )

        def arrived(f, r):
            remote(
                spot(f, r),
                spot(f, r),
                gsend_sem.at[g, f, r - 1],
                grecv_sem.at[g, f, r - 1],
                flip(me, 1, bits),
            ).wait_recv()

        back = [order[::-1] for order in orders]
        for f in range(FLOWS):
            span = slice(f * per * BLK, (f + 1) * per * BLK)
            part = lax.dot_general(
                solved, basis[span], (((1,), (1,)), ((), ())), preferred_element_type=F32
            )
            start_ref[lines, span] = part
            for i in range(per):
                spot_of = me * own_blocks + f * per + i
                gat[spot_of] = part[:, i * BLK : (i + 1) * BLK].astype(BF16)
            for b in back[f]:
                go(double_copy(f, 0, b))
        yield
        known = [[] for _ in range(FLOWS)]
        for u in range(1, bits):
            for f in range(FLOWS):
                last = 1 << back[f][u - 1]
                fresh = [last] + [r ^ last for r in known[f]]
                for r in fresh:
                    arrived(f, r)
                known[f] = known[f] + fresh
                for r in known[f]:
                    go(double_copy(f, r, back[f][u]))
            yield
        for f in range(FLOWS):
            last = 1 << back[f][bits - 1]
            for r in [last] + [r ^ last for r in known[f]]:
                arrived(f, r)

        def second(s, carry):
            picked = [gat[target[s * per_sub + j]] for j in range(per_sub)]
            held = jnp.concatenate(picked, axis=1)
            add_runs(s, jnp.dot(held, operators[s], preferred_element_type=F32), lines)
            return carry

        for part in range(PARTS):
            lax.fori_loop(subs * part // PARTS, subs * (part + 1) // PARTS, second, 0)
            yield
        settle()
        for t in range(bits):
            halve_step(t)
            yield
        for f in range(FLOWS):
            part = total(f, 0, bits)
            for i in range(per):
                blk = f * per + i
                span = slice(blk * BLK, (blk + 1) * BLK)
                resid_ref[lines, span] = dual[lines, span] - part[i] * weight[blk : blk + 1, :]
        settle()

    interleave(group(g) for g in range(GROUPS))


def per_device(n, loads, operators, owner, dual_block, scale_index, basis, coarse):
    subs, columns, rows_in = loads.shape
    local_rows = basis.shape[0]
    own_blocks = local_rows // BLK
    duals = n * own_blocks
    target = owner.reshape(-1) * own_blocks + dual_block
    nblocks = target.shape[0]
    key = jnp.concatenate([target, jnp.arange(duals, dtype=jnp.int32)])
    bound = jnp.minimum(jnp.arange(nblocks + duals, dtype=jnp.int32), nblocks)
    places = jnp.arange(nblocks, dtype=jnp.int32)
    hit = (key[:, None] == target[None, :]) & (places[None, :] < bound[:, None])
    found = jnp.max(jnp.where(hit, places[None, :], -1), axis=1)
    links = jnp.where(found < 0, nblocks, found)
    scale = scale_index.reshape(own_blocks, BLK)
    per = own_blocks // FLOWS
    dirs = coarse.shape[0]
    height = columns // GROUPS
    across = min(n, dirs // BLK)
    piece = (height * across // n, dirs // across)
    vmem = pl.BlockSpec(memory_space=pltpu.VMEM)
    smem = pl.BlockSpec(memory_space=pltpu.SMEM)
    hbm = pl.BlockSpec(memory_space=pl.ANY)
    dma = pltpu.SemaphoreType.DMA
    out = jax.ShapeDtypeStruct((columns, local_rows), F32)
    return pl.pallas_call(
        functools.partial(kernel, n),
        out_shape=(out, out),
        in_specs=[smem, smem, vmem] + [hbm] * 4,
        out_specs=(vmem, vmem),
        scratch_shapes=[
            pltpu.VMEM(loads.shape, BF16),
            pltpu.VMEM(operators.shape, BF16),
            pltpu.VMEM(basis.shape, BF16),
            pltpu.VMEM(coarse.shape, BF16),
            pltpu.VMEM((nblocks + 1, columns, BLK), F32),
            tuple(pltpu.VMEM((duals, height, BLK), BF16) for _ in range(GROUPS)),
            pltpu.VMEM((GROUPS, FLOWS, n - 1, per, height, BLK), BF16),
            pltpu.VMEM((GROUPS, FLOWS, n - 1, per, height, BLK), BF16),
            pltpu.VMEM((GROUPS, n) + piece, BF16),
            pltpu.VMEM((GROUPS, n - 1) + piece, BF16),
            pltpu.VMEM((GROUPS, n) + piece, BF16),
            pltpu.VMEM((columns, local_rows), F32),
            dma((3,)),
            dma((subs,)),
            dma((GROUPS, FLOWS, n - 1)),
            dma((GROUPS, FLOWS, n - 1)),
            dma((GROUPS, n - 1)),
            dma((GROUPS, n - 1)),
            dma((GROUPS, n - 1)),
            dma((GROUPS, n - 1)),
            dma((GROUPS, FLOWS, n - 1)),
            dma((GROUPS, FLOWS, n - 1)),
        ],
        compiler_params=pltpu.CompilerParams(
            collective_id=0, has_side_effects=True, vmem_limit_bytes=VMEM_LIMIT
        ),
        name="feti",
    )(target, links, scale, loads, operators, basis, coarse)


def solution(mesh):
    return jax.shard_map(
        functools.partial(per_device, mesh.shape["sub"]),
        mesh=mesh,
        in_specs=(
            P("sub", "rep", None),
            P("sub", None, None),
            P("sub", None),
            P("sub"),
            P("sub"),
            P("sub", None),
            P(),
        ),
        out_specs=(P("rep", "sub"), P("rep", "sub")),
        check_vma=False,
    )
```

time: 68 us -> 69.7 us (1.025)
  Pallas kernels: 62 us -> 63.6 us
    pallas_call x1, Pallas kernels: 62 us -> 63.6 us  [per_device(): pl.pallas_call(functools.partial(kernel, n), out_shape=(out, out), in_spe...]
where the time goes in v3:
time: 69.7 us; the launch traced here: 69.5 us
  Pallas kernels  63.6 us (91%)
  local copies, waits for them, and re-layouts  3.75 us (5%)
  other arithmetic  1.42 us (2%)
    pallas_call x1, Pallas kernels, per_device(): pl.pallas_call(functools.partial(kernel, n), out_shape=(out, out), in_spe...  63.6 us
    unnamed x4, local copies, waits for them, and re-layouts  3.75 us

profile of v3, /device:TPU:0, one launch (start us, length us, event | category | flops | bytes accessed | tf_op | source)
XLA Modules:
  0.0 69.5 jit_solution(1598884259468928711)
XLA Ops:
  0.6 0.7 bitcast_add_fusion.target
  1.3 0.0 copy-start
  1.3 0.1 pad_add_fusion
  1.4 0.1 select_reduce_fusion
  1.5 0.6 compare_select_fusion.links
  2.1 0.0 copy-done
  2.1 63.6 %feti.1 = (f32[64,2048]{1,0:T(8,128)}, f32[64,2048]{1,0:T(8,128)}) custom-call(s32[64]{0:T(128)} %copy-done, s32[192]{0:T(256)} %compare_select_fusion.links, s32[16,128]{1,0:T(8,128)} %bitcast.3, bf16[8,64,1024]{2,1,0:T(8,128)(2,1)} %loads_hbm.1, bf16[8,1024,1024]{2,1,0:T(8,128)(2,1)} %operators_hbm.1, bf16[2048,1024]{1,0:T(8,128)(2,1)} %basis_hbm.1, ...), custom_call_target="tpu_custom_call" | custom-call | tf_op jit(solution)/shard_map/feti/pallas_call | solution.py:349
  65.7 1.9 %copy.11 = f32[64,2048]{1,0:T(8,128)} copy(f32[64,2048]{1,0:T(8,128)} %get-tuple-element.6) | data formatting | bytes 1048576
  67.6 1.9 %copy.12 = f32[64,2048]{1,0:T(8,128)} copy(f32[64,2048]{1,0:T(8,128)} %get-tuple-element.7) | data formatting | bytes 1048576
  (1 shorter events, 0.0 us)
Async XLA Ops:
  1.3 0.7 %copy-start = (s32[64]{0:T(128)}, s32[64]{0:T(128)S(1)}, u32[]{:S(2)}) copy-start(s32[64]{0:T(128)S(1)} %bitcast_add_fusion.target) | copy-start | bytes 772

commit v4 on v2

--- a/solution.py
+++ b/solution.py
@@ -315,6 +315,11 @@
         copy.wait_send()
 
 
+def hand_over(start_in, resid_in, start_out, resid_out):
+    start_out[...] = start_in[...]
+    resid_out[...] = resid_in[...]
+
+
 def per_device(n, loads, operators, owner, dual_block, scale_index, basis, coarse):
     subs, columns, rows_in = loads.shape
     local_rows = basis.shape[0]
@@ -338,7 +343,7 @@
     hbm = pl.BlockSpec(memory_space=pl.ANY)
     dma = pltpu.SemaphoreType.DMA
     out = jax.ShapeDtypeStruct((columns, local_rows), F32)
-    return pl.pallas_call(
+    results = pl.pallas_call(
         functools.partial(kernel, n),
         out_shape=(out, out),
         in_specs=[smem, smem, vmem] + [hbm] * 4,
@@ -373,6 +378,15 @@
         ),
         name="feti",
     )(target, links, scale, loads, operators, basis, coarse)
+    tile = pl.BlockSpec((columns // 2, local_rows), lambda i: (i, 0))
+    return pl.pallas_call(
+        hand_over,
+        out_shape=(out, out),
+        grid=(2,),
+        in_specs=[tile, tile],
+        out_specs=(tile, tile),
+        name="hand_over",
+    )(*results)
 
 
 def solution(mesh):

time: 68 us -> 66.3 us (0.975)
  local copies, waits for them, and re-layouts: 3.75 us -> 0.01 us
  Pallas kernels: 62 us -> 64 us
    unnamed x4 -> x2, local copies, waits for them, and re-layouts: 3.75 us -> 0.01 us
    pallas_call x0 -> x1, Pallas kernels: none -> 2.04 us  [per_device(): pl.pallas_call(hand_over, out_shape=(out, out), grid=(2,), in_specs=[tile...]
where the time goes in v4:
time: 66.3 us; the launch traced here: 66.1 us
  Pallas kernels  64 us (97%)
  other arithmetic  1.42 us (2%)
    pallas_call x1, Pallas kernels, per_device(): pl.pallas_call(functools.partial(kernel, n), out_shape=(out, out), in_spe...  62 us
    pallas_call x1, Pallas kernels, per_device(): pl.pallas_call(hand_over, out_shape=(out, out), grid=(2,), in_specs=[tile...  2.04 us

profile of v4, /device:TPU:0, one launch (start us, length us, event | category | flops | bytes accessed | tf_op | source)
XLA Modules:
  0.0 66.1 jit_solution(10077355881075852180)
XLA Ops:
  0.6 0.7 %bitcast_add_fusion.target = s32[64]{0:T(128)S(1)} fusion(s32[64]{0:T(128)} %param.10, s32[64,1]{0,1:T(1,128)} %param.9), kind=kLoop, calls=%fused_computation.6 | loop fusion | flops 128 | bytes 768 | tf_op jit(solution)/shard_map/add | solution.py:328
  1.3 0.0 copy-start
  1.3 0.1 pad_add_fusion
  1.4 0.1 select_reduce_fusion
  1.5 0.6 compare_select_fusion.links
  2.1 0.0 copy-done
  2.1 62.0 %feti.1 = (f32[64,2048]{1,0:T(8,128)}, f32[64,2048]{1,0:T(8,128)}) custom-call(s32[64]{0:T(128)} %copy-done, s32[192]{0:T(256)} %compare_select_fusion.links, s32[16,128]{1,0:T(8,128)} %bitcast.3, bf16[8,64,1024]{2,1,0:T(8,128)(2,1)} %loads_hbm.1, bf16[8,1024,1024]{2,1,0:T(8,128)(2,1)} %operators_hbm.1, bf16[2048,1024]{1,0:T(8,128)(2,1)} %basis_hbm.1, ...), custom_call_target="tpu_custom_call" | custom-call | tf_op jit(solution)/shard_map/feti/pallas_call | solution.py:346
  64.0 2.0 %hand_over.1 = (f32[64,2048]{1,0:T(8,128)}, f32[64,2048]{1,0:T(8,128)}) custom-call(f32[64,2048]{1,0:T(8,128)} %get-tuple-element.4.start_in, f32[64,2048]{1,0:T(8,128)} %get-tuple-element.5.resid_in), custom_call_target="tpu_custom_call" | custom-call | tf_op jit(solution)/shard_map/hand_over/pallas_call | solution.py:382
  (1 shorter events, 0.0 us)
Async XLA Ops:
  1.3 0.7 %copy-start = (s32[64]{0:T(128)}, s32[64]{0:T(128)S(1)}, u32[]{:S(2)}) copy-start(s32[64]{0:T(128)S(1)} %bitcast_add_fusion.target) | copy-start | bytes 772
